TPU v7x, 32 devices: a whole 2x2x4 slice. The times are simulated.
32 devices in a mesh: rows: 16 (over z, y, core), cent: 2 (over x).
Axes of the slice: x: 2, y: 2, z: 4, core: 2. Of those that a mesh axis runs over, the one named last changes fastest.
Arguments:
- vectors: bfloat16 [32768, 1024], P('rows'), may hold values from -40 to 40
- centroids: bfloat16 [1024, 4096], P('rows', 'cent'), may hold values from -8 to 8
Outputs:
- centroid_sums: float32 [1024, 4096], P('rows', 'cent')
All inputs are finite; a program needn't handle non-finite values.
Results may differ from a plain program's by a relative error of at most 0.0017.
Values may be sent and summed in bfloat16 or wider, within the bound.
A program may use at most 64 MiB of HBM per device.

v0:
```python
import math

import jax
import jax.numpy as jnp
from jax import lax
from jax.sharding import PartitionSpec as P

K = 4096
ITERS = 3


sharpness = 3.0


def on_device(vectors, centroids):
    row_count = vectors.shape[0]
    width = vectors.shape[1]
    window = vectors
    scores = jnp.dot(
        window,
        lax.all_gather(centroids, "rows", axis=0, tiled=True),
        preferred_element_type=jnp.float32,
    )
    scores = scores * (sharpness / math.sqrt(width))
    row_top = lax.pmax(jnp.max(scores, axis=1), "cent")
    numerator = jnp.exp(scores - row_top[:, None])
    row_total = lax.psum(jnp.sum(numerator, axis=1), "cent")
    balanced = numerator / row_total[:, None]
    target = row_count * lax.axis_size("rows") / K
    for iteration in range(ITERS):
        column_sum = jnp.sum(balanced, axis=0)
        column_mass = lax.psum(column_sum, "rows")
        column_scale = target / column_mass
        balanced = balanced * column_scale[None, :]
        row_mass = lax.psum(jnp.sum(balanced, axis=1), "cent")
        balanced = balanced / row_mass[:, None]
    weights = balanced.astype(jnp.bfloat16)
    factor = K / (row_count * lax.axis_size("rows"))
    window = vectors
    mine = lax.psum_scatter(
        lax.dot_general(
            window, weights, (((0,), (0,)), ((), ())), preferred_element_type=jnp.float32
        ),
        "rows",
        scatter_dimension=0,
        tiled=True,
    )
    return mine * factor


def solution(mesh):
    return jax.shard_map(
        on_device,
        mesh=mesh,
        in_specs=(P("rows", None), P("rows", "cent")),
        out_specs=P("rows", "cent"),
        check_vma=False,
    )
```

profile of v0, /device:TPU:1, one launch (start us, length us, event | category | flops | bytes accessed | tf_op | source)
XLA Modules:
  0.0 385.2 jit_solution(11446826470317669100)
XLA Ops:
  6.5 0.0 all-gather.2.cloned.1.call-start
  6.5 0.7 all-gather.2.cloned.1.call-update
  7.3 0.0 reduce-scatter.4.cloned.1.call-start
  7.3 55.1 %all-gather.2.cloned.1.call-done = bf16[1024,2048]{1,0:T(8,128)(2,1)} async-done(((bf16[64,2048]{1,0:T(8,128)(2,1)}), bf16[1024,2048]{1,0:T(8,128)(2,1)}) %all-gather.2.cloned.1.call-update) | async-done | bytes 4194320 | tf_op jit(solution)/shard_map/all_gather | solution.py:21
  62.4 15.2 %multiply_reduce_fusion.3 = (f32[2048]{0:T(1024)S(1)}, f32[2048,2048]{0,1:T(8,128)}) fusion(bf16[2048,1024]{1,0:T(8,128)(2,1)} %param.2, bf16[1024,2048]{1,0:T(8,128)(2,1)} %all-gather.2.cloned.1.call-done), kind=kOutput, calls=%fused_computation.7 | convolution fusion | flops 8598321152 | bytes 25174016 | tf_op jit(solution)/shard_map/dot_general | solution.py:19
  77.6 3.8 pmax.7
  81.4 8.5 %fusion.1 = f32[2048]{0:T(1024)S(1)} fusion(f32[2048,2048]{0,1:T(8,128)} %get-tuple-element.8, f32[2048]{0:T(1024)S(1)} %pmax.7), kind=kLoop, calls=%fused_computation.9 | loop fusion | flops 12580864 | bytes 16793600 | tf_op jit(solution)/shard_map/reduce_sum | solution.py:27
  90.0 3.8 psum.49
  93.8 7.7 %fusion.4 = f32[2048]{0:T(1024)S(1)} fusion(f32[2048]{0:T(1024)S(1)} %psum.49, f32[2048]{0:T(1024)S(1)} %pmax.7, f32[2048,2048]{0,1:T(8,128)} %get-tuple-element.8), kind=kLoop, calls=%fused_computation.16 | loop fusion | flops 16775168 | bytes 16801792 | tf_op jit(solution)/shard_map/reduce_sum | solution.py:31
  101.5 31.9 %psum.50 = f32[2048]{0:T(1024)S(1)} all-reduce(f32[2048]{0:T(1024)S(1)} %fusion.4), channel_id=1, replica_groups=mesh['rows'=16,'cent'=2] {'rows'}, use_global_device_ids=true, to_apply=%region_5.0 | all-reduce | flops 2048 | bytes 16384 | tf_op jit(solution)/shard_map/psum | solution.py:32
  133.5 8.1 %multiply_reduce_fusion.2 = f32[2048]{0:T(1024)S(1)} fusion(f32[2048]{0:T(1024)S(1)} %broadcast_divide_fusion.2, f32[2048]{0:T(1024)S(1)} %psum.49, f32[2048]{0:T(1024)S(1)} %pmax.7, f32[2048,2048]{0,1:T(8,128)} %get-tuple-element.8), kind=kLoop, calls=%fused_computation.6 | loop fusion | flops 20969472 | bytes 16809984 | tf_op jit(solution)/shard_map/reduce_sum | solution.py:35
  141.6 3.8 psum.51
  145.4 13.1 %fusion.6 = (f32[2048]{0:T(1024)S(1)}, f32[2048,2048]{0,1:T(8,128)}) fusion(f32[2048]{0:T(1024)S(1)} %psum.51, f32[2048]{0:T(1024)S(1)} %broadcast_divide_fusion.2, f32[2048]{0:T(1024)S(1)} %psum.49, f32[2048]{0:T(1024)S(1)} %pmax.7, f32[2048,2048]{0,1:T(8,128)} %get-tuple-element.8), kind=kLoop, calls=%fused_computation.18 | loop fusion | flops 25163776 | bytes 33595392 | tf_op jit(solution)/shard_map/reduce_sum | solution.py:31
  158.5 31.4 %psum.52 = f32[2048]{0:T(1024)S(1)} all-reduce(f32[2048]{0:T(1024)S(1)} %get-tuple-element.5), channel_id=1, replica_groups=mesh['rows'=16,'cent'=2] {'rows'}, use_global_device_ids=true, to_apply=%region_9.0 | all-reduce | flops 2048 | bytes 16384 | tf_op jit(solution)/shard_map/psum | solution.py:32
  189.9 6.9 %multiply_reduce_fusion.1 = f32[2048]{0:T(1024)S(1)} fusion(f32[2048,2048]{0,1:T(8,128)} %get-tuple-element.6, f32[2048]{0:T(1024)S(1)} %broadcast_divide_fusion.1), kind=kLoop, calls=%fused_computation.4 | loop fusion | flops 8386560 | bytes 16793600 | tf_op jit(solution)/shard_map/reduce_sum | solution.py:35
  196.9 3.8 psum.53
  200.7 7.1 %fusion.5 = f32[2048]{0:T(1024)S(1)} fusion(f32[2048]{0:T(1024)S(1)} %psum.53, f32[2048,2048]{0,1:T(8,128)} %get-tuple-element.6, f32[2048]{0:T(1024)S(1)} %broadcast_divide_fusion.1), kind=kLoop, calls=%fused_computation.17 | loop fusion | flops 12580864 | bytes 16801792 | tf_op jit(solution)/shard_map/reduce_sum | solution.py:31
  207.8 31.2 %psum.54 = f32[2048]{0:T(1024)S(1)} all-reduce(f32[2048]{0:T(1024)S(1)} %fusion.5), channel_id=1, replica_groups=mesh['rows'=16,'cent'=2] {'rows'}, use_global_device_ids=true, to_apply=%region_13.0 | all-reduce | flops 2048 | bytes 16384 | tf_op jit(solution)/shard_map/psum | solution.py:32
  239.0 7.2 %multiply_reduce_fusion = f32[2048]{0:T(1024)S(1)} fusion(f32[2048]{0:T(1024)S(1)} %broadcast_divide_fusion, f32[2048]{0:T(1024)S(1)} %psum.53, f32[2048,2048]{0,1:T(8,128)} %get-tuple-element.6, f32[2048]{0:T(1024)S(1)} %broadcast_divide_fusion.1), kind=kLoop, calls=%fused_computation.2 | loop fusion | flops 16775168 | bytes 16809984 | tf_op jit(solution)/shard_map/reduce_sum | solution.py:35
  246.2 3.8 psum.55
  250.1 15.7 %fusion.3 = f32[1024,2048]{0,1:T(8,128)} fusion(bf16[2048,1024]{1,0:T(8,128)(2,1)} %param.2, f32[2048]{0:T(1024)S(1)} %psum.55, f32[2048]{0:T(1024)S(1)} %broadcast_divide_fusion, f32[2048,2048]{0,1:T(8,128)} %get-tuple-element.6, f32[2048]{0:T(1024)S(1)} %psum.53, f32[2048]{0:T(1024)S(1)} %broadcast_divide_fusion.1), kind=kOutput, calls=%fused_computation.11 | convolution fusion | flops 8610906112 | bytes 29392896 | tf_op jit(solution)/shard_map/dot_general | solution.py:41
  265.7 9.1 %copy.6 = f32[1024,2048]{1,0:T(8,128)} copy(f32[1024,2048]{0,1:T(8,128)} %fusion.3) | data formatting | bytes 16777216
  274.9 0.0 reduce-scatter.4.cloned.1.call-update
  274.9 101.6 %reduce-scatter.4.cloned.1.call-done = f32[64,2048]{1,0:T(8,128)} async-done(((f32[1024,2048]{1,0:T(8,128)}), f32[64,2048]{1,0:T(8,128)}) %reduce-scatter.4.cloned.1.call-update) | async-done | bytes 524304 | tf_op jit(solution)/shard_map/reduce_scatter | solution.py:40
  376.5 1.9 broadcast_multiply_fusion
  (3 shorter events, 0.0 us)
Async XLA Ops:
  6.5 55.8 %all-gather.2.cloned.1.call-start = ((), (), s32[]{:S(2)}) async-start(), calls=%async_computation.1 | async-start | bytes 4456448 | tf_op jit(solution)/shard_map/all_gather | solution.py:21
  7.3 369.2 %reduce-scatter.4.cloned.1.call-start = ((), (), s32[]{:S(2)}) async-start(), calls=%async_computation.2 | async-start | bytes 8912896 | tf_op jit(solution)/shard_map/reduce_scatter | solution.py:40
Sparse Core Ops, SparseCore 0:
  9.5 52.8 all-gather.1
  275.0 101.4 reduce-scatter.3
where the time goes:
time: 387 us; the launch traced here: 385 us
  waiting for transfers between devices  157 us (41%)
  blocking collectives  114 us (29%)
  other arithmetic  60.6 us (16%)
  matrix products  30.9 us (8%)
  between operations  13.5 us (3%)
  local copies, waits for them, and re-layouts  9.11 us (2%)
    reduce_scatter x1, waiting for transfers between devices, on_device(): lax.psum_scatter(lax.dot_general(window, weights, (((0,), (0,)), ((), ())...  102 us
    psum x3, blocking collectives, on_device(): column_mass = lax.psum(column_sum, 'rows')  94.4 us
    all_gather x1, waiting for transfers between devices, on_device(): lax.all_gather(centroids, 'rows', axis=0, tiled=True)  55.1 us
    reduce_sum x3, other arithmetic, on_device(): column_sum = jnp.sum(balanced, axis=0)  27.9 us
    reduce_sum x3, other arithmetic, on_device(): row_mass = lax.psum(jnp.sum(balanced, axis=1), 'cent')  22.3 us
    dot_general x1, matrix products, on_device(): lax.dot_general(window, weights, (((0,), (0,)), ((), ())), preferred_elem...  15.7 us
    dot_general x1, matrix products, on_device(): jnp.dot(window, lax.all_gather(centroids, 'rows', axis=0, tiled=True), pr...  15.2 us
    psum x3, blocking collectives, on_device(): row_mass = lax.psum(jnp.sum(balanced, axis=1), 'cent')  11.5 us
  transfers between devices with their start and end apart: 2, of which 2 were waited for; matrix products, arithmetic and copies ran while one was open for 0% of the time, Pallas kernels for 0%

commit v1 on v0

v1 whole, which is shorter than its diff:
```python
import functools
import math

import jax
import jax.numpy as jnp
from jax import lax
from jax.experimental import pallas as pl
from jax.experimental.pallas import tpu as pltpu
from jax.sharding import PartitionSpec as P

ITERS = 3
SHARPNESS = 3.0
MESH = pl.DeviceIdType.MESH
LANES = 128


def position_of(row, ring):
    chips = ring // 2
    chip, core = row // 2, row % 2
    far, near = chip // 2, chip % 2
    place = far + near * (chips - 1 - 2 * far)
    return place * 2 + core


def row_at(position, ring):
    chips = ring // 2
    place, core = position // 2, position % 2
    half = chips // 2
    near = place // half
    far = place + near * (chips - 1 - 2 * place)
    return (far * 2 + near) * 2 + core


def kernel(ring, groups, total_rows, columns_total, vec_ref, cen_ref, out_ref, cen_full, vec_t, bal, wts, rows_b,
           part, row_x, col_x, sum_in, ag_send, ag_recv, row_send, row_recv, col_send, col_recv, rs_send, rs_recv):
    rows, width = vec_ref.shape
    depth, cols = cen_ref.shape
    me = lax.axis_index("rows")
    my_group = lax.axis_index("cent")
    pos = position_of(me, ring)
    right = row_at((pos + 1) % ring, ring)
    left = row_at((pos + ring - 1) % ring, ring)
    neighbours = (right, left)
    chunks = min(4, cols // LANES)
    cw = cols // chunks

    barrier = pltpu.get_barrier_semaphore()

    def greet(o, carry):
        pl.semaphore_signal(barrier, inc=1, device_id={"rows": (me + o) % ring}, device_id_type=MESH)
        return carry

    lax.fori_loop(1, ring, greet, 0)
    for o in range(1, groups):
        pl.semaphore_signal(barrier, inc=1, device_id={"cent": (my_group + o) % groups}, device_id_type=MESH)

    tile = 256

    mine = pl.ds(pl.multiple_of(me * depth, depth), depth)
    cen_full[mine, :] = cen_ref[...]
    pl.semaphore_wait(barrier, ring - 1 + groups - 1)

    steps = (ring // 2, ring // 2 - 1)

    def gather_copy(way, step, chunk):
        source = (pos + ring - step) % ring if way == 0 else (pos + step) % ring
        block = row_at(source, ring)
        view = cen_full.at[pl.ds(pl.multiple_of(block * depth, depth), depth), pl.ds(chunk * cw, cw)]
        return pltpu.make_async_remote_copy(
            src_ref=view, dst_ref=view, send_sem=ag_send.at[way, step, chunk], recv_sem=ag_recv.at[way, step, chunk],
            device_id={"rows": neighbours[way]}, device_id_type=MESH)

    def gather_arrival(way, step, chunk):
        source = (pos + ring - step - 1) % ring if way == 0 else (pos + step + 1) % ring
        block = row_at(source, ring)
        view = cen_full.at[pl.ds(pl.multiple_of(block * depth, depth), depth), pl.ds(chunk * cw, cw)]
        return pltpu.make_async_remote_copy(
            src_ref=view, dst_ref=view, send_sem=ag_send.at[way, step, chunk], recv_sem=ag_recv.at[way, step, chunk],
            device_id={"rows": neighbours[way]}, device_id_type=MESH)

    for chunk in range(chunks):
        for way in range(2):
            gather_copy(way, 0, chunk).start()

    def turn(t, carry):
        at = pl.ds(pl.multiple_of(t * tile, tile), tile)
        vec_t[:, at] = vec_ref[at, :].T
        return carry

    lax.fori_loop(0, rows // tile, turn, 0)

    def gather_step(step, carry):
        for chunk in range(chunks):
            for way in range(2):
                gather_arrival(way, step - 1, chunk).wait_recv()
                gather_copy(way, step, chunk).start()
        return carry

    lax.fori_loop(1, steps[1], gather_step, 0)
    last = steps[1]
    for chunk in range(chunks):
        gather_arrival(0, last - 1, chunk).wait_recv()
        gather_copy(0, last, chunk).start()
        gather_arrival(1, last - 1, chunk).wait_recv()
    for chunk in range(chunks):
        gather_arrival(0, last, chunk).wait_recv()

    scale = SHARPNESS / math.sqrt(width)
    strips = cols // LANES

    def to_lanes(op):
        return op(part[...].T, axis=0, keepdims=True)

    def to_rows(vector):
        rows_b[...] = jnp.broadcast_to(vector, (LANES, rows)).T

    def score(t, carry):
        at = pl.ds(pl.multiple_of(t * tile, tile), tile)
        top = None
        for chunk in range(chunks):
            s = jnp.dot(vec_ref[at, :], cen_full[:, chunk * cw:(chunk + 1) * cw],
                        preferred_element_type=jnp.float32) * scale
            bal[at, chunk * cw:(chunk + 1) * cw] = s
            for j in range(cw // LANES):
                piece = s[:, j * LANES:(j + 1) * LANES]
                top = piece if top is None else jnp.maximum(top, piece)
        part[at, :] = jnp.broadcast_to(jnp.max(top, axis=1, keepdims=True), (tile, LANES))
        return carry

    lax.fori_loop(0, rows // tile, score, 0)
    top = to_lanes(jnp.max)
    row_x[0, 0, 0:1, :] = top

    small = 32

    def exponent(t, carry):
        at = pl.ds(pl.multiple_of(t * small, small), small)
        m = part[at, :]
        acc = None
        for j in range(strips):
            lanes = slice(j * LANES, (j + 1) * LANES)
            e = jnp.exp(bal[at, lanes] - m)
            bal[at, lanes] = e
            acc = e if acc is None else acc + e
        part[at, :] = acc
        return carry

    lax.fori_loop(0, rows // small, exponent, 0)
    row_x[0, 0, 1:2, :] = to_lanes(jnp.sum)

    def row_copy(turn_, o):
        return pltpu.make_async_remote_copy(
            src_ref=row_x.at[turn_, 0], dst_ref=row_x.at[turn_, o], send_sem=row_send.at[turn_, o],
            recv_sem=row_recv.at[turn_, o], device_id={"cent": (my_group + o) % groups}, device_id_type=MESH)

    def col_copy(turn_, o):
        return pltpu.make_async_remote_copy(
            src_ref=col_x.at[turn_, 0], dst_ref=col_x.at[turn_, o], send_sem=col_send.at[turn_, o],
            recv_sem=col_recv.at[turn_, o], device_id={"rows": (me + o) % ring}, device_id_type=MESH)

    def swap_rows(turn_):
        for o in range(1, groups):
            row_copy(turn_, o).start()
        for o in range(1, groups):
            row_copy(turn_, o).wait_recv()

    swap_rows(0)
    tops = [row_x[0, o, 0:1, :] for o in range(groups)]
    sums = [row_x[0, o, 1:2, :] for o in range(groups)]
    highest = functools.reduce(jnp.maximum, tops)
    total = functools.reduce(jnp.add, [s * jnp.exp(m - highest) for s, m in zip(sums, tops)])
    to_rows(jnp.exp(tops[0] - highest) / total)

    target = total_rows / columns_total

    def column_pass(column_scale):
        def body(t, accs):
            at = pl.ds(pl.multiple_of(t * small, small), small)
            r = rows_b[at, :]
            new = []
            for j in range(strips):
                lanes = slice(j * LANES, (j + 1) * LANES)
                b = bal[at, lanes]
                if column_scale is not None:
                    b = b * column_scale[:, lanes]
                b = b * r
                bal[at, lanes] = b
                folded = accs[j]
                for q in range(small // 8):
                    folded = folded + b[q * 8:(q + 1) * 8, :]
                new.append(folded)
            return tuple(new)

        accs = lax.fori_loop(0, rows // small, body, tuple(jnp.zeros((8, LANES), jnp.float32) for _ in range(strips)))
        return [jnp.sum(a, axis=0, keepdims=True) for a in accs]

    def row_pass(column_scale):
        def body(t, carry):
            at = pl.ds(pl.multiple_of(t * small, small), small)
            acc = None
            for j in range(strips):
                lanes = slice(j * LANES, (j + 1) * LANES)
                b = bal[at, lanes] * column_scale[:, lanes]
                acc = b if acc is None else acc + b
            part[at, :] = acc
            return carry

        lax.fori_loop(0, rows // small, body, 0)
        return to_lanes(jnp.sum)

    column_scale = None
    for it in range(ITERS):
        sums = column_pass(column_scale)
        for j in range(strips):
            col_x[it, 0, :, j * LANES:(j + 1) * LANES] = sums[j]

        def send(o, carry, it=it):
            col_copy(it, o).start()
            return carry

        def receive(o, acc, it=it):
            col_copy(it, o).wait_recv()
            return acc + col_x[it, o]

        lax.fori_loop(1, ring, send, 0)
        mass = lax.fori_loop(1, ring, receive, col_x[it, 0])
        column_scale = target / mass
        row_x[it + 1, 0, 0:1, :] = row_pass(column_scale)
        swap_rows(it + 1)
        mass = functools.reduce(jnp.add, [row_x[it + 1, o, 0:1, :] for o in range(groups)])
        to_rows(1.0 / mass)

    def weigh(t, carry):
        at = pl.ds(pl.multiple_of(t * small, small), small)
        r = rows_b[at, :]
        for j in range(strips):
            lanes = slice(j * LANES, (j + 1) * LANES)
            wts[at, lanes] = (bal[at, lanes] * column_scale[:, lanes] * r).astype(jnp.bfloat16)
        return carry

    lax.fori_loop(0, rows // small, weigh, 0)

    dt = min(256, width)
    factor = columns_total / total_rows

    def multiply(t, carry):
        at = pl.ds(pl.multiple_of(t * dt, dt), dt)
        for chunk in range(chunks):
            lanes = slice(chunk * cw, (chunk + 1) * cw)
            bal[at, lanes] = jnp.dot(vec_t[at, :], wts[:, lanes], preferred_element_type=jnp.float32) * factor
        return carry

    lax.fori_loop(0, width // dt, multiply, 0)

    def block_at(way, step):
        where = (pos + 2 * ring - 1 - step) % ring if way == 0 else (pos + 1 + step) % ring
        return pl.ds(pl.multiple_of(row_at(where, ring) * depth, depth), depth)

    pieces = chunks
    half = pieces // 2

    def sum_copy(piece, step):
        way = 0 if piece < half else 1
        lanes = pl.ds(piece * cw, cw)
        return pltpu.make_async_remote_copy(
            src_ref=bal.at[block_at(way, step), lanes], dst_ref=sum_in.at[step, piece],
            send_sem=rs_send.at[step, piece], recv_sem=rs_recv.at[step, piece],
            device_id={"rows": neighbours[way]}, device_id_type=MESH)

    order = [p + w * half for p in range(half) for w in range(2)]
    for piece in order:
        sum_copy(piece, 0).start()

    def sum_step(step, carry):
        for piece in order:
            way = 0 if piece < half else 1
            lanes = slice(piece * cw, (piece + 1) * cw)
            sum_copy(piece, step - 1).wait_recv()
            at = block_at(way, step)
            bal[at, lanes] = bal[at, lanes] + sum_in[step - 1, piece]
            sum_copy(piece, step).start()
        return carry

    lax.fori_loop(1, ring - 1, sum_step, 0)
    for piece in order:
        lanes = slice(piece * cw, (piece + 1) * cw)
        sum_copy(piece, ring - 2).wait_recv()
        out_ref[:, lanes] = bal[mine, lanes] + sum_in[ring - 2, piece]

    def drain_gather(step, carry):
        for chunk in range(chunks):
            for way in range(2):
                gather_copy(way, step, chunk).wait_send()
        return carry

    lax.fori_loop(0, steps[1], drain_gather, 0)
    for chunk in range(chunks):
        gather_copy(0, steps[1], chunk).wait_send()
    for turn_ in range(ITERS + 1):
        for o in range(1, groups):
            row_copy(turn_, o).wait_send()

    def drain_columns(o, carry):
        for it in range(ITERS):
            col_copy(it, o).wait_send()
        return carry

    lax.fori_loop(1, ring, drain_columns, 0)

    def drain_sums(step, carry):
        for piece in order:
            sum_copy(piece, step).wait_send()
        return carry

    lax.fori_loop(0, ring - 1, drain_sums, 0)


def solution(mesh):
    ring, groups = mesh.shape["rows"], mesh.shape["cent"]

    def on_device(vectors, centroids):
        rows, width = vectors.shape
        depth, cols = centroids.shape
        chunks = min(4, cols // LANES)
        f32, bf16 = jnp.float32, jnp.bfloat16
        dma = pltpu.SemaphoreType.DMA
        return pl.pallas_call(
            functools.partial(kernel, ring, groups, rows * ring, cols * groups),
            out_shape=jax.ShapeDtypeStruct((depth, cols), f32),
            in_specs=[pl.BlockSpec(memory_space=pltpu.VMEM)] * 2,
            out_specs=pl.BlockSpec(memory_space=pltpu.VMEM),
            scratch_shapes=[
                pltpu.VMEM((width, cols), bf16),
                pltpu.VMEM((width, rows), bf16),
                pltpu.VMEM((max(rows, width), cols), f32),
                pltpu.VMEM((rows, cols), bf16),
                pltpu.VMEM((rows, LANES), f32),
                pltpu.VMEM((rows, LANES), f32),
                pltpu.VMEM((ITERS + 1, groups, 2, rows), f32),
                pltpu.VMEM((ITERS, ring, 1, cols), f32),
                pltpu.VMEM((ring - 1, chunks, depth, cols // chunks), f32),
                dma((2, ring // 2, chunks)),
                dma((2, ring // 2, chunks)),
                dma((ITERS + 1, groups)),
                dma((ITERS + 1, groups)),
                dma((ITERS, ring)),
                dma((ITERS, ring)),
                dma((ring - 1, chunks)),
                dma((ring - 1, chunks)),
            ],
            compiler_params=pltpu.CompilerParams(
                collective_id=0, has_side_effects=True, vmem_limit_bytes=66 * 1000 * 1000),
        )(vectors, centroids)

    return jax.shard_map(
        on_device,
        mesh=mesh,
        in_specs=(P("rows", None), P("rows", "cent")),
        out_specs=P("rows", "cent"),
        check_vma=False,
    )
```

time: 387 us -> 149 us (0.39)
  waiting for transfers between devices: 157 us -> 0 us
  Pallas kernels: 0 us -> 147 us
  blocking collectives: 114 us -> 0 us
  other arithmetic: 60.6 us -> 0 us
  matrix products: 30.9 us -> 0 us
  between operations: 13.5 us -> 0.01 us
  local copies, waits for them, and re-layouts: 9.11 us -> 1.87 us
    pallas_call x0 -> x1, Pallas kernels: none -> 147 us  [on_device(): pl.pallas_call(functools.partial(kernel, ring, groups, rows * ring, cols...]
    psum x7 -> x0, blocking collectives: 110 us -> none  [the longest x3 94.4 us: on_device(): column_mass = lax.psum(column_sum, 'rows')]
    reduce_scatter x1 -> x0, waiting for transfers between devices: 102 us -> none  [on_device(): lax.psum_scatter(lax.dot_general(window, weights, (((0,), (0,)), ((), ())...]
    reduce_sum x7 -> x0, other arithmetic: 58.7 us -> none  [the longest x3 27.9 us: on_device(): column_sum = jnp.sum(balanced, axis=0)]
    all_gather x1 -> x0, waiting for transfers between devices: 55.1 us -> none  [on_device(): lax.all_gather(centroids, 'rows', axis=0, tiled=True)]
    dot_general x2 -> x0, matrix products: 30.9 us -> none  [the longest x1 15.7 us: on_device(): lax.dot_general(window, weights, (((0,), (0,)), ((), ())), preferred_elem...]
    unnamed x1, local copies, waits for them, and re-layouts: 9.11 us -> 1.87 us
  transfers between devices with their start and end apart: 2 -> 0, of which waited for: 2 -> 0; matrix products, arithmetic and copies ran while one was open for 0% -> 0% of each run, Pallas kernels for 0% -> 0%
where the time goes in v1:
time: 149 us
  Pallas kernels  147 us (99%)
  local copies, waits for them, and re-layouts  1.87 us (1%)
    pallas_call x1, Pallas kernels, on_device(): pl.pallas_call(functools.partial(kernel, ring, groups, rows * ring, cols...  147 us

profile of v1, /device:TPU:1, one launch (start us, length us, event | category | flops | bytes accessed | tf_op | source)
XLA Modules:
  0.0 148.6 jit_solution(7633453365482778854)
XLA Ops:
  0.0 146.7 %shard_map.28 = f32[64,2048]{1,0:T(8,128)} custom-call(bf16[2048,1024]{1,0:T(8,128)(2,1)} %vec_ref.1, bf16[64,2048]{1,0:T(8,128)(2,1)} %cen_ref.1), custom_call_target="tpu_custom_call" | custom-call | tf_op jit(solution)/shard_map/pallas_call | solution.py:327
  146.7 1.9 %copy.4 = f32[64,2048]{1,0:T(8,128)} copy(f32[64,2048]{1,0:T(8,128)} %shard_map.28) | data formatting | bytes 1048576

commit v2 on v1

--- a/solution.py
+++ b/solution.py
@@ -12,6 +12,14 @@
 SHARPNESS = 3.0
 MESH = pl.DeviceIdType.MESH
 LANES = 128
+SHARES = 2
+
+
+def short_steps(ring):
+    steps = 0
+    while (steps + 1) * (steps + 2) / 2 <= 0.65 * ring:
+        steps += 1
+    return steps
 
 
 def position_of(row, ring):
@@ -31,8 +39,8 @@
     return (far * 2 + near) * 2 + core
 
 
-def kernel(ring, groups, total_rows, columns_total, vec_ref, cen_ref, out_ref, cen_full, vec_t, bal, wts, rows_b,
-           part, row_x, col_x, sum_in, ag_send, ag_recv, row_send, row_recv, col_send, col_recv, rs_send, rs_recv):
+def kernel(ring, groups, shorts, total_rows, columns_total, vec_ref, cen_ref, out_ref, cen_full, vec_t, bal, wts, rows_b,
+           part, row_x, col_x, short_out, short_in, sum_in, ag_send, ag_recv, row_send, row_recv, col_send, col_recv, rs_send, rs_recv):
     rows, width = vec_ref.shape
     depth, cols = cen_ref.shape
     me = lax.axis_index("rows")
@@ -108,11 +116,16 @@
     scale = SHARPNESS / math.sqrt(width)
     strips = cols // LANES
 
-    def to_lanes(op):
-        return op(part[...].T, axis=0, keepdims=True)
-
-    def to_rows(vector):
-        rows_b[...] = jnp.broadcast_to(vector, (LANES, rows)).T
+    share = rows // SHARES
+
+    def rows_of(part_):
+        return pl.ds(part_ * share, share)
+
+    def to_lanes(op, part_):
+        return op(part[rows_of(part_), :].T, axis=0, keepdims=True)
+
+    def to_rows(vector, part_):
+        rows_b[rows_of(part_), :] = jnp.broadcast_to(vector, (LANES, share)).T
 
     def score(t, carry):
         at = pl.ds(pl.multiple_of(t * tile, tile), tile)
@@ -128,10 +141,8 @@
         return carry
 
     lax.fori_loop(0, rows // tile, score, 0)
-    top = to_lanes(jnp.max)
-    row_x[0, 0, 0:1, :] = top
-
     small = 32
+    per_share = share // small
 
     def exponent(t, carry):
         at = pl.ds(pl.multiple_of(t * small, small), small)
@@ -145,35 +156,47 @@
         part[at, :] = acc
         return carry
 
-    lax.fori_loop(0, rows // small, exponent, 0)
-    row_x[0, 0, 1:2, :] = to_lanes(jnp.sum)
-
-    def row_copy(turn_, o):
+    def row_copy(turn_, part_, o):
         return pltpu.make_async_remote_copy(
-            src_ref=row_x.at[turn_, 0], dst_ref=row_x.at[turn_, o], send_sem=row_send.at[turn_, o],
-            recv_sem=row_recv.at[turn_, o], device_id={"cent": (my_group + o) % groups}, device_id_type=MESH)
+            src_ref=row_x.at[turn_, part_, 0], dst_ref=row_x.at[turn_, part_, o],
+            send_sem=row_send.at[turn_, part_, o], recv_sem=row_recv.at[turn_, part_, o],
+            device_id={"cent": (my_group + o) % groups}, device_id_type=MESH)
 
     def col_copy(turn_, o):
         return pltpu.make_async_remote_copy(
             src_ref=col_x.at[turn_, 0], dst_ref=col_x.at[turn_, o], send_sem=col_send.at[turn_, o],
             recv_sem=col_recv.at[turn_, o], device_id={"rows": (me + o) % ring}, device_id_type=MESH)
 
-    def swap_rows(turn_):
+    def send_rows(turn_, part_):
         for o in range(1, groups):
-            row_copy(turn_, o).start()
+            row_copy(turn_, part_, o).start()
+
+    def receive_rows(turn_, part_):
         for o in range(1, groups):
-            row_copy(turn_, o).wait_recv()
-
-    swap_rows(0)
-    tops = [row_x[0, o, 0:1, :] for o in range(groups)]
-    sums = [row_x[0, o, 1:2, :] for o in range(groups)]
-    highest = functools.reduce(jnp.maximum, tops)
-    total = functools.reduce(jnp.add, [s * jnp.exp(m - highest) for s, m in zip(sums, tops)])
-    to_rows(jnp.exp(tops[0] - highest) / total)
+            row_copy(turn_, part_, o).wait_recv()
+
+    for part_ in range(SHARES):
+        row_x[0, part_, 0, 0:1, :] = to_lanes(jnp.max, part_)
+        lax.fori_loop(part_ * per_share, (part_ + 1) * per_share, exponent, 0)
+        row_x[0, part_, 0, 1:2, :] = to_lanes(jnp.sum, part_)
+        send_rows(0, part_)
+
+    def softmax_rows(part_):
+        receive_rows(0, part_)
+        tops = [row_x[0, part_, o, 0:1, :] for o in range(groups)]
+        sums = [row_x[0, part_, o, 1:2, :] for o in range(groups)]
+        highest = functools.reduce(jnp.maximum, tops)
+        total = functools.reduce(jnp.add, [s * jnp.exp(m - highest) for s, m in zip(sums, tops)])
+        to_rows(jnp.exp(tops[0] - highest) / total, part_)
+
+    def balance_rows(turn_, part_):
+        receive_rows(turn_, part_)
+        mass = functools.reduce(jnp.add, [row_x[turn_, part_, o, 0:1, :] for o in range(groups)])
+        to_rows(1.0 / mass, part_)
 
     target = total_rows / columns_total
 
-    def column_pass(column_scale):
+    def column_pass(column_scale, part_, accs):
         def body(t, accs):
             at = pl.ds(pl.multiple_of(t * small, small), small)
             r = rows_b[at, :]
@@ -191,10 +214,9 @@
                 new.append(folded)
             return tuple(new)
 
-        accs = lax.fori_loop(0, rows // small, body, tuple(jnp.zeros((8, LANES), jnp.float32) for _ in range(strips)))
-        return [jnp.sum(a, axis=0, keepdims=True) for a in accs]
-
-    def row_pass(column_scale):
+        return lax.fori_loop(part_ * per_share, (part_ + 1) * per_share, body, accs)
+
+    def row_pass(column_scale, part_):
         def body(t, carry):
             at = pl.ds(pl.multiple_of(t * small, small), small)
             acc = None
@@ -205,14 +227,20 @@
             part[at, :] = acc
             return carry
 
-        lax.fori_loop(0, rows // small, body, 0)
-        return to_lanes(jnp.sum)
+        lax.fori_loop(part_ * per_share, (part_ + 1) * per_share, body, 0)
+        return to_lanes(jnp.sum, part_)
 
     column_scale = None
     for it in range(ITERS):
-        sums = column_pass(column_scale)
+        accs = tuple(jnp.zeros((8, LANES), jnp.float32) for _ in range(strips))
+        for part_ in range(SHARES):
+            if it == 0:
+                softmax_rows(part_)
+            else:
+                balance_rows(it, part_)
+            accs = column_pass(column_scale, part_, accs)
         for j in range(strips):
-            col_x[it, 0, :, j * LANES:(j + 1) * LANES] = sums[j]
+            col_x[it, 0, :, j * LANES:(j + 1) * LANES] = jnp.sum(accs[j], axis=0, keepdims=True)
 
         def send(o, carry, it=it):
             col_copy(it, o).start()
@@ -225,10 +253,9 @@
         lax.fori_loop(1, ring, send, 0)
         mass = lax.fori_loop(1, ring, receive, col_x[it, 0])
         column_scale = target / mass
-        row_x[it + 1, 0, 0:1, :] = row_pass(column_scale)
-        swap_rows(it + 1)
-        mass = functools.reduce(jnp.add, [row_x[it + 1, o, 0:1, :] for o in range(groups)])
-        to_rows(1.0 / mass)
+        for part_ in range(SHARES):
+            row_x[it + 1, part_, 0, 0:1, :] = row_pass(column_scale, part_)
+            send_rows(it + 1, part_)
 
     def weigh(t, carry):
         at = pl.ds(pl.multiple_of(t * small, small), small)
@@ -238,19 +265,12 @@
             wts[at, lanes] = (bal[at, lanes] * column_scale[:, lanes] * r).astype(jnp.bfloat16)
         return carry
 
-    lax.fori_loop(0, rows // small, weigh, 0)
+    for part_ in range(SHARES):
+        balance_rows(ITERS, part_)
+        lax.fori_loop(part_ * per_share, (part_ + 1) * per_share, weigh, 0)
 
     dt = min(256, width)
     factor = columns_total / total_rows
-
-    def multiply(t, carry):
-        at = pl.ds(pl.multiple_of(t * dt, dt), dt)
-        for chunk in range(chunks):
-            lanes = slice(chunk * cw, (chunk + 1) * cw)
-            bal[at, lanes] = jnp.dot(vec_t[at, :], wts[:, lanes], preferred_element_type=jnp.float32) * factor
-        return carry
-
-    lax.fori_loop(0, width // dt, multiply, 0)
 
     def block_at(way, step):
         where = (pos + 2 * ring - 1 - step) % ring if way == 0 else (pos + 1 + step) % ring
@@ -262,30 +282,60 @@
     def sum_copy(piece, step):
         way = 0 if piece < half else 1
         lanes = pl.ds(piece * cw, cw)
+        if step < shorts:
+            source, target_ = short_out.at[step, piece], short_in.at[step, piece]
+        else:
+            source, target_ = bal.at[block_at(way, step), lanes], sum_in.at[step - shorts, piece]
         return pltpu.make_async_remote_copy(
-            src_ref=bal.at[block_at(way, step), lanes], dst_ref=sum_in.at[step, piece],
-            send_sem=rs_send.at[step, piece], recv_sem=rs_recv.at[step, piece],
+            src_ref=source, dst_ref=target_, send_sem=rs_send.at[step, piece], recv_sem=rs_recv.at[step, piece],
             device_id={"rows": neighbours[way]}, device_id_type=MESH)
 
+    def arrived(piece, step):
+        if step < shorts:
+            return short_in[step, piece].astype(jnp.float32)
+        return sum_in[step - shorts, piece]
+
+    def advance(piece, step):
+        way = 0 if piece < half else 1
+        lanes = slice(piece * cw, (piece + 1) * cw)
+        at = mine if step == ring - 1 else block_at(way, step)
+        value = bal[at, lanes]
+        if step > 0:
+            sum_copy(piece, step - 1).wait_recv()
+            value = value + arrived(piece, step - 1)
+        if step == ring - 1:
+            out_ref[:, lanes] = value
+            return
+        if step < shorts:
+            short_out[step, piece] = value.astype(jnp.bfloat16)
+        elif step > 0:
+            bal[at, lanes] = value
+        sum_copy(piece, step).start()
+
     order = [p + w * half for p in range(half) for w in range(2)]
-    for piece in order:
-        sum_copy(piece, 0).start()
-
-    def sum_step(step, carry):
-        for piece in order:
-            way = 0 if piece < half else 1
-            lanes = slice(piece * cw, (piece + 1) * cw)
-            sum_copy(piece, step - 1).wait_recv()
-            at = block_at(way, step)
-            bal[at, lanes] = bal[at, lanes] + sum_in[step - 1, piece]
-            sum_copy(piece, step).start()
-        return carry
-
-    lax.fori_loop(1, ring - 1, sum_step, 0)
+    done = {}
+    tiles = width // dt
     for piece in order:
         lanes = slice(piece * cw, (piece + 1) * cw)
-        sum_copy(piece, ring - 2).wait_recv()
-        out_ref[:, lanes] = bal[mine, lanes] + sum_in[ring - 2, piece]
+
+        def multiply(t, carry, lanes=lanes):
+            at = pl.ds(pl.multiple_of(t * dt, dt), dt)
+            bal[at, lanes] = jnp.dot(vec_t[at, :], wts[:, lanes], preferred_element_type=jnp.float32) * factor
+            return carry
+
+        for first in range(0, tiles, 2):
+            lax.fori_loop(first, min(first + 2, tiles), multiply, 0)
+            for other in done:
+                if done[other] < ring - 1:
+                    advance(other, done[other])
+                    done[other] += 1
+        advance(piece, 0)
+        done[piece] = 1
+    while min(done.values()) < ring:
+        for piece in order:
+            if done[piece] < ring:
+                advance(piece, done[piece])
+                done[piece] += 1
 
     def drain_gather(step, carry):
         for chunk in range(chunks):
@@ -297,8 +347,9 @@
     for chunk in range(chunks):
         gather_copy(0, steps[1], chunk).wait_send()
     for turn_ in range(ITERS + 1):
-        for o in range(1, groups):
-            row_copy(turn_, o).wait_send()
+        for part_ in range(SHARES):
+            for o in range(1, groups):
+                row_copy(turn_, part_, o).wait_send()
 
     def drain_columns(o, carry):
         for it in range(ITERS):
@@ -307,12 +358,9 @@
 
     lax.fori_loop(1, ring, drain_columns, 0)
 
-    def drain_sums(step, carry):
+    for step in range(ring - 1):
         for piece in order:
             sum_copy(piece, step).wait_send()
-        return carry
-
-    lax.fori_loop(0, ring - 1, drain_sums, 0)
 
 
 def solution(mesh):
@@ -322,10 +370,11 @@
         rows, width = vectors.shape
         depth, cols = centroids.shape
         chunks = min(4, cols // LANES)
+        shorts = short_steps(ring)
         f32, bf16 = jnp.float32, jnp.bfloat16
         dma = pltpu.SemaphoreType.DMA
         return pl.pallas_call(
-            functools.partial(kernel, ring, groups, rows * ring, cols * groups),
+            functools.partial(kernel, ring, groups, shorts, rows * ring, cols * groups),
             out_shape=jax.ShapeDtypeStruct((depth, cols), f32),
             in_specs=[pl.BlockSpec(memory_space=pltpu.VMEM)] * 2,
             out_specs=pl.BlockSpec(memory_space=pltpu.VMEM),
@@ -336,13 +385,15 @@
                 pltpu.VMEM((rows, cols), bf16),
                 pltpu.VMEM((rows, LANES), f32),
                 pltpu.VMEM((rows, LANES), f32),
-                pltpu.VMEM((ITERS + 1, groups, 2, rows), f32),
+                pltpu.VMEM((ITERS + 1, SHARES, groups, 2, rows // SHARES), f32),
                 pltpu.VMEM((ITERS, ring, 1, cols), f32),
-                pltpu.VMEM((ring - 1, chunks, depth, cols // chunks), f32),
+                pltpu.VMEM((shorts, chunks, depth, cols // chunks), bf16),
+                pltpu.VMEM((shorts, chunks, depth, cols // chunks), bf16),
+                pltpu.VMEM((ring - 1 - shorts, chunks, depth, cols // chunks), f32),
                 dma((2, ring // 2, chunks)),
                 dma((2, ring // 2, chunks)),
-                dma((ITERS + 1, groups)),
-                dma((ITERS + 1, groups)),
+                dma((ITERS + 1, SHARES, groups)),
+                dma((ITERS + 1, SHARES, groups)),
                 dma((ITERS, ring)),
                 dma((ITERS, ring)),
                 dma((ring - 1, chunks)),

time: 149 us -> 150 us (level)
    pallas_call x1, Pallas kernels: 147 us -> 148 us  [on_device(): pl.pallas_call(functools.partial(kernel, ring, groups, shorts, rows * rin...]
where the time goes in v2:
time: 150 us
  Pallas kernels  148 us (99%)
  local copies, waits for them, and re-layouts  1.87 us (1%)
    pallas_call x1, Pallas kernels, on_device(): pl.pallas_call(functools.partial(kernel, ring, groups, shorts, rows * rin...  148 us

profile of v2, /device:TPU:1, one launch (start us, length us, event | category | flops | bytes accessed | tf_op | source)
XLA Modules:
  0.0 150.2 jit_solution(1669212805442599379)
XLA Ops:
  0.0 148.3 %shard_map.28 = f32[64,2048]{1,0:T(8,128)} custom-call(bf16[2048,1024]{1,0:T(8,128)(2,1)} %vec_ref.1, bf16[64,2048]{1,0:T(8,128)(2,1)} %cen_ref.1), custom_call_target="tpu_custom_call" | custom-call | tf_op jit(solution)/shard_map/pallas_call | solution.py:376
  148.3 1.9 %copy.4 = f32[64,2048]{1,0:T(8,128)} copy(f32[64,2048]{1,0:T(8,128)} %shard_map.28) | data formatting | bytes 1048576

commit v3 on v2

--- a/solution.py
+++ b/solution.py
@@ -323,12 +323,7 @@
             bal[at, lanes] = jnp.dot(vec_t[at, :], wts[:, lanes], preferred_element_type=jnp.float32) * factor
             return carry
 
-        for first in range(0, tiles, 2):
-            lax.fori_loop(first, min(first + 2, tiles), multiply, 0)
-            for other in done:
-                if done[other] < ring - 1:
-                    advance(other, done[other])
-                    done[other] += 1
+        lax.fori_loop(0, tiles, multiply, 0)
         advance(piece, 0)
         done[piece] = 1
     while min(done.values()) < ring:

time: 150 us -> 143 us (0.953)
  Pallas kernels: 148 us -> 141 us
    pallas_call x1, Pallas kernels: 148 us -> 141 us  [on_device(): pl.pallas_call(functools.partial(kernel, ring, groups, shorts, rows * rin...]
where the time goes in v3:
time: 143 us; the launch traced here: 142 us
  Pallas kernels  141 us (99%)
  local copies, waits for them, and re-layouts  1.87 us (1%)
    pallas_call x1, Pallas kernels, on_device(): pl.pallas_call(functools.partial(kernel, ring, groups, shorts, rows * rin...  141 us

profile of v3, /device:TPU:1, one launch (start us, length us, event | category | flops | bytes accessed | tf_op | source)
XLA Modules:
  0.0 142.5 jit_solution(8646943408000959196)
XLA Ops:
  0.0 140.6 %shard_map.28 = f32[64,2048]{1,0:T(8,128)} custom-call(bf16[2048,1024]{1,0:T(8,128)(2,1)} %vec_ref.1, bf16[64,2048]{1,0:T(8,128)(2,1)} %cen_ref.1), custom_call_target="tpu_custom_call" | custom-call | tf_op jit(solution)/shard_map/pallas_call | solution.py:371
  140.6 1.9 %copy.4 = f32[64,2048]{1,0:T(8,128)} copy(f32[64,2048]{1,0:T(8,128)} %shard_map.28) | data formatting | bytes 1048576
